TPU v7x, 512 devices: a whole 4x8x8 slice. The times are simulated.
512 devices in a mesh: chan: 8 (over z), sx: 8 (over x, core), sy: 8 (over y).
Axes of the slice: x: 4, y: 8, z: 8, core: 2. Of those that a mesh axis runs over, the one named last changes fastest.
Arguments:
- volume: bfloat16 [8, 64, 64, 256], P('sx', 'sy', None, 'chan'), may hold values from -6 to 6
- kernel: bfloat16 [27, 256, 256], P(None, 'chan'), may hold values from -0.078125 to 0.078125
- grad_out: bfloat16 [8, 64, 64, 256], P('sx', 'sy', None, 'chan'), may hold values from -6 to 6
Outputs:
- out: bfloat16 [8, 64, 64, 256], P('sx', 'sy', None, 'chan')
- grad_input: bfloat16 [8, 64, 64, 256], P('sx', 'sy', None, 'chan')
- grad_kernel: float32 [27, 256, 256], P(None, 'chan')
All inputs are finite; a program needn't handle non-finite values.
Results may differ from a plain program's by a relative error of at most 0.0015.
Values may be sent and summed in bfloat16 or wider, within the bound.
No kernel may reach another device: no remote copies, remote signals or barrier semaphores. Data moves between devices by JAX's collectives and lax.ppermute only.
A program may use at most 64 MiB of HBM per device.

v0:
```python
import math
import jax
import jax.numpy as jnp
from jax import lax
from jax.sharding import PartitionSpec as P


def padded_2(shard, sides, width):
    for axis, dim in sides:
        count, length = (lax.axis_size(axis), shard.shape[dim])
        up = [(i, (i + 1) % count) for i in range(count - 1)]
        down = [(j, i) for i, j in up]
        last = lax.slice_in_dim(shard, length - width, length, axis=dim)
        leading = lax.slice_in_dim(shard, 0, width, axis=dim)
        before = lax.ppermute(last, axis, up)
        after = lax.ppermute(leading, axis, down)
        shard = jnp.concatenate([before, shard, after], axis=dim)
    return shard


def body(volume, kernel, grad_out):
    size_x, size_y, size_z, own_in = volume.shape
    total_out = kernel.shape[2]
    cells = size_x * size_y * size_z
    rim = padded_2(volume, (("sx", 0), ("sy", 1)), 1)
    padded = jnp.pad(rim, ((0, 0), (0, 0), (1, 1), (0, 0)))
    offsets = [(index // 9, index // 3 % 3, index % 3) for index in range(27)]
    partial_out = jnp.zeros((cells, total_out), jnp.float32)
    for index in range(27):
        a, b, e = offsets[index]
        window = padded[a : a + size_x, b : b + size_y, e : e + size_z].reshape(cells, own_in)
        partial_out = partial_out + jnp.dot(
            window, kernel[index], preferred_element_type=jnp.float32
        )
    partial_out = partial_out.reshape(size_x, size_y, size_z, total_out)
    out = lax.psum_scatter(partial_out, "chan", scatter_dimension=3, tiled=True).astype(
        jnp.bfloat16
    )
    grad_full = lax.all_gather(grad_out, "chan", axis=3, tiled=True)
    grad_rimmed = padded_2(grad_full, (("sx", 0), ("sy", 1)), 1)
    grad_padded = jnp.pad(grad_rimmed, ((0, 0), (0, 0), (1, 1), (0, 0)))
    flat_grad = grad_full.reshape(cells, total_out)
    back = jnp.zeros((cells, own_in), jnp.float32)
    kernel_terms = []
    for index in range(27):
        a, b, e = offsets[index]
        window = grad_padded[
            2 - a : 2 - a + size_x, 2 - b : 2 - b + size_y, 2 - e : 2 - e + size_z
        ].reshape(cells, total_out)
        back = back + lax.dot_general(
            window, kernel[index], (((1,), (1,)), ((), ())), preferred_element_type=jnp.float32
        )
        in_window = padded[a : a + size_x, b : b + size_y, e : e + size_z].reshape(cells, own_in)
        kernel_terms.append(
            lax.dot_general(
                in_window, flat_grad, (((0,), (0,)), ((), ())), preferred_element_type=jnp.float32
            )
        )
    grad_input = back.reshape(size_x, size_y, size_z, own_in).astype(jnp.bfloat16)
    local_kernel = jnp.stack(kernel_terms)
    summed = lax.psum(local_kernel, ("sx", "sy"))
    all_cells = cells * lax.axis_size("sx") * lax.axis_size("sy")
    grad_kernel = summed / jnp.float32(math.sqrt(all_cells))
    return (out, grad_input, grad_kernel)


def solution(mesh):
    return jax.shard_map(
        body,
        mesh=mesh,
        in_specs=(P("sx", "sy", None, "chan"), P(None, "chan", None), P("sx", "sy", None, "chan")),
        out_specs=(P("sx", "sy", None, "chan"), P("sx", "sy", None, "chan"), P(None, "chan", None)),
        check_vma=False,
    )
```

profile of v0, /device:TPU:25, one launch (start us, length us, event | category | flops | bytes accessed | tf_op | source)
XLA Modules:
  0.0 342.9 jit_solution(3898932481704692713)
XLA Ops:
  8.1 3.7 %collective-permute-start = (bf16[1,8,64,32]{2,3,1,0:T(8,128)(2,1)}, bf16[1,8,64,32]{2,3,1,0:T(8,128)(2,1)S(1)}, u32[]{:S(2)}, u32[]{:S(2)}) collective-permute-start(bf16[1,8,64,32]{2,3,1,0:T(8,128)(2,1)} %param.3), channel_id=1, source_target_pairs={{0,8},{8,16},{16,24},{24,32},{32,40},{40,48},{48,56},{1,9},{9,17},... | collective-permute-start | bytes 98312 | tf_op jit(solution)/shard_map/ppermute | solution.py:15
  11.7 1.9 collective-permute-start.1
  15.5 2.1 collective-permute-done.1
  17.6 2.1 collective-permute-start.3
  19.7 4.4 %collective-permute-start.2 = (bf16[3,1,64,32]{2,3,1,0:T(8,128)(2,1)S(1)}, bf16[3,1,64,32]{2,3,1,0:T(8,128)(2,1)S(1)}, u32[]{:S(2)}, u32[]{:S(2)}) collective-permute-start(bf16[3,1,64,32]{2,3,1,0:T(8,128)(2,1)S(1)} %get-tuple-element.68), channel_id=1, source_target_pairs={{0,1},{1,2},{2,3},{3,4},{4,5},{5,6},{6,7},{8,9},{9,10},{10,11},{11... | collective-permute-start | bytes 36872 | tf_op jit(solution)/shard_map/ppermute | solution.py:15
  24.1 26.2 %all_gather.3 = bf16[1,8,64,256]{2,1,0,3:T(8,128)(2,1)S(1)} all-gather(bf16[1,8,64,32]{2,1,0,3:T(8,128)(2,1)S(1)} %copy.98), channel_id=1, replica_groups=mesh['chan'=8,'sx'=8,'sy'=8] {'chan'}, dimensions={3}, use_global_device_ids=true | all-gather | bytes 294912 | tf_op jit(solution)/shard_map/all_gather | solution.py:39
  50.6 5.5 %collective-permute-start.5 = (bf16[1,8,64,256]{3,2,1,0:T(8,128)(2,1)S(1)}, bf16[1,8,64,256]{3,2,1,0:T(8,128)(2,1)S(1)}, u32[]{:S(2)}, u32[]{:S(2)}) collective-permute-start(bf16[1,8,64,256]{3,2,1,0:T(8,128)(2,1)S(1)} %copy.99), channel_id=1, source_target_pairs={{8,0},{16,8},{24,16},{32,24},{40,32},{48,40},{56,48},{9,1},{17,9},... | collective-permute-start | bytes 786440 | tf_op jit(solution)/shard_map/ppermute | solution.py:16
  56.1 4.7 %collective-permute-start.4 = (bf16[1,8,64,256]{3,2,1,0:T(8,128)(2,1)S(1)}, bf16[1,8,64,256]{3,2,1,0:T(8,128)(2,1)S(1)}, u32[]{:S(2)}, u32[]{:S(2)}) collective-permute-start(bf16[1,8,64,256]{3,2,1,0:T(8,128)(2,1)S(1)} %copy.99), channel_id=1, source_target_pairs={{0,8},{8,16},{16,24},{24,32},{32,40},{40,48},{48,56},{1,9},{9,17},... | collective-permute-start | bytes 786440 | tf_op jit(solution)/shard_map/ppermute | solution.py:15
  63.9 1.1 fusion.241
  67.0 1.4 pad_maximum_fusion.13
  73.0 1.5 copy.76
  74.5 1.6 reshape.329
  76.1 1.5 copy.77
  77.6 1.6 reshape.330
  79.2 1.5 copy.78
  80.6 1.6 reshape.331
  82.2 1.5 copy.79
  83.7 1.6 reshape.332
  85.9 1.6 reshape.333
  88.1 1.6 reshape.334
  90.3 1.6 reshape.335
  91.9 1.5 copy.84
  93.4 1.6 reshape.337
  95.0 1.5 copy.85
  96.4 1.6 reshape.338
  98.7 1.6 reshape.339
  100.9 1.6 reshape.340
  102.4 1.5 copy.88
  103.9 1.6 reshape.341
  106.1 1.6 reshape.342
  107.7 1.5 copy.90
  109.2 1.6 reshape.343
  110.7 1.5 copy.91
  112.2 1.6 reshape.344
  114.5 1.6 reshape.347
  116.8 0.9 fusion.35
  119.3 0.9 fusion.32
  121.9 0.9 fusion.29
  124.4 0.9 fusion.26
  126.9 0.9 fusion.23
  129.4 0.9 fusion.20
  146.8 1.9 collective-permute-start.7
  148.7 4.8 %collective-permute-start.6 = (bf16[3,1,64,256]{3,2,1,0:T(8,128)(2,1)S(1)}, bf16[3,1,64,256]{3,2,1,0:T(8,128)(2,1)S(1)}, u32[]{:S(2)}, u32[]{:S(2)}) collective-permute-start(bf16[3,1,64,256]{3,2,1,0:T(8,128)(2,1)S(1)} %get-tuple-element.39), channel_id=1, source_target_pairs={{0,1},{1,2},{2,3},{3,4},{4,5},{5,6},{6,7},{8,9},{9,10},{10,11},{11... | collective-permute-start | bytes 294920 | tf_op jit(solution)/shard_map/ppermute | solution.py:15
  153.8 1.3 copy.97
  155.8 0.9 fusion.240
  162.8 168.9 %all-reduce.4.cloned.1.call-done = f32[27,32,256]{2,1,0:T(8,128)} async-done(((f32[27,32,256]{2,1,0:T(8,128)}), f32[27,32,256]{2,1,0:T(8,128)}) %all-reduce.4.cloned.1.call-update) | async-done | bytes 884752 | tf_op jit(solution)/shard_map/psum | solution.py:61
  331.7 2.2 broadcast_multiply_fusion
  333.9 1.5 convert_element_type.21
  (205 shorter events, 48.3 us)
Async XLA Ops:
  8.0 52.8 %copy-start.4 = (bf16[1,8,64,32]{2,3,1,0:T(8,128)(2,1)S(1)}, bf16[1,8,64,32]{2,3,1,0:T(8,128)(2,1)}, u32[]{:S(2)}) copy-start(bf16[1,8,64,32]{2,3,1,0:T(8,128)(2,1)} %param.3) | copy-start | bytes 98308
  8.0 323.7 %all-reduce.4.cloned.1.call-start = ((), (), s32[]{:S(2)}) async-start(), calls=%async_computation.2 | async-start | bytes 1769472 | tf_op jit(solution)/shard_map/psum | solution.py:61
  8.1 6.5 %collective-permute-start = (bf16[1,8,64,32]{2,3,1,0:T(8,128)(2,1)}, bf16[1,8,64,32]{2,3,1,0:T(8,128)(2,1)S(1)}, u32[]{:S(2)}, u32[]{:S(2)}) collective-permute-start(bf16[1,8,64,32]{2,3,1,0:T(8,128)(2,1)} %param.3), channel_id=1, source_target_pairs={{0,8},{8,16},{16,24},{24,32},{32,40},{40,48},{48,56},{1,9},{9,17},... | collective-permute-start | bytes 98312 | tf_op jit(solution)/shard_map/ppermute | solution.py:15
  11.7 5.8 %collective-permute-start.1 = (bf16[1,8,64,32]{2,3,1,0:T(8,128)(2,1)}, bf16[1,8,64,32]{2,3,1,0:T(8,128)(2,1)S(1)}, u32[]{:S(2)}, u32[]{:S(2)}) collective-permute-start(bf16[1,8,64,32]{2,3,1,0:T(8,128)(2,1)} %param.3), channel_id=1, source_target_pairs={{8,0},{16,8},{24,16},{32,24},{40,32},{48,40},{56,48},{9,1},{17,9},... | collective-permute-start | bytes 98312 | tf_op jit(solution)/shard_map/ppermute | solution.py:16
  14.6 47.1 %copy-start.8 = (bf16[1,8,64,32]{2,3,1,0:T(8,128)(2,1)}, bf16[1,8,64,32]{2,3,1,0:T(8,128)(2,1)S(1)}, u32[]{:S(2)}) copy-start(bf16[1,8,64,32]{2,3,1,0:T(8,128)(2,1)S(1)} %collective-permute-done) | copy-start | bytes 98308
  17.5 45.0 %copy-start.6 = (bf16[1,8,64,32]{2,3,1,0:T(8,128)(2,1)}, bf16[1,8,64,32]{2,3,1,0:T(8,128)(2,1)S(1)}, u32[]{:S(2)}) copy-start(bf16[1,8,64,32]{2,3,1,0:T(8,128)(2,1)S(1)} %collective-permute-done.1) | copy-start | bytes 98308
  17.6 44.9 %collective-permute-start.3 = (bf16[3,1,64,32]{2,3,1,0:T(8,128)(2,1)S(1)}, bf16[3,1,64,32]{2,3,1,0:T(8,128)(2,1)S(1)}, u32[]{:S(2)}, u32[]{:S(2)}) collective-permute-start(bf16[3,1,64,32]{2,3,1,0:T(8,128)(2,1)S(1)} %get-tuple-element.69), channel_id=1, source_target_pairs={{1,0},{2,1},{3,2},{4,3},{5,4},{6,5},{7,6},{9,8},{10,9},{11,10},{12... | collective-permute-start | bytes 36872 | tf_op jit(solution)/shard_map/ppermute | solution.py:16
  19.7 42.9 %collective-permute-start.2 = (bf16[3,1,64,32]{2,3,1,0:T(8,128)(2,1)S(1)}, bf16[3,1,64,32]{2,3,1,0:T(8,128)(2,1)S(1)}, u32[]{:S(2)}, u32[]{:S(2)}) collective-permute-start(bf16[3,1,64,32]{2,3,1,0:T(8,128)(2,1)S(1)} %get-tuple-element.68), channel_id=1, source_target_pairs={{0,1},{1,2},{2,3},{3,4},{4,5},{5,6},{6,7},{8,9},{9,10},{10,11},{11... | collective-permute-start | bytes 36872 | tf_op jit(solution)/shard_map/ppermute | solution.py:15
  50.6 96.1 %collective-permute-start.5 = (bf16[1,8,64,256]{3,2,1,0:T(8,128)(2,1)S(1)}, bf16[1,8,64,256]{3,2,1,0:T(8,128)(2,1)S(1)}, u32[]{:S(2)}, u32[]{:S(2)}) collective-permute-start(bf16[1,8,64,256]{3,2,1,0:T(8,128)(2,1)S(1)} %copy.99), channel_id=1, source_target_pairs={{8,0},{16,8},{24,16},{32,24},{40,32},{48,40},{56,48},{9,1},{17,9},... | collective-permute-start | bytes 786440 | tf_op jit(solution)/shard_map/ppermute | solution.py:16
  56.1 90.7 %collective-permute-start.4 = (bf16[1,8,64,256]{3,2,1,0:T(8,128)(2,1)S(1)}, bf16[1,8,64,256]{3,2,1,0:T(8,128)(2,1)S(1)}, u32[]{:S(2)}, u32[]{:S(2)}) collective-permute-start(bf16[1,8,64,256]{3,2,1,0:T(8,128)(2,1)S(1)} %copy.99), channel_id=1, source_target_pairs={{0,8},{8,16},{16,24},{24,32},{32,40},{40,48},{48,56},{1,9},{9,17},... | collective-permute-start | bytes 786440 | tf_op jit(solution)/shard_map/ppermute | solution.py:15
  62.5 0.6 copy-start.36
  63.1 0.6 copy-start.37
  63.9 2.3 copy-start
  68.5 0.6 copy-start.2
  68.5 18.9 %copy-start.14 = (bf16[1,8,64,32]{2,3,1,0:T(8,128)(2,1)S(1)}, bf16[1,8,64,32]{2,3,1,0:T(8,128)(2,1)}, u32[]{:S(2)}) copy-start(bf16[1,8,64,32]{2,3,1,0:T(8,128)(2,1)} %get-tuple-element.51) | copy-start | bytes 98308
  68.5 21.2 %copy-start.13 = (bf16[1,8,64,32]{2,3,1,0:T(8,128)(2,1)S(1)}, bf16[1,8,64,32]{2,3,1,0:T(8,128)(2,1)}, u32[]{:S(2)}) copy-start(bf16[1,8,64,32]{2,3,1,0:T(8,128)(2,1)} %get-tuple-element.50) | copy-start | bytes 98308
  74.5 25.7 %copy-start.12 = (bf16[1,8,64,32]{2,3,1,0:T(8,128)(2,1)S(1)}, bf16[1,8,64,32]{2,3,1,0:T(8,128)(2,1)}, u32[]{:S(2)}) copy-start(bf16[1,8,64,32]{2,3,1,0:T(8,128)(2,1)} %get-tuple-element.47) | copy-start | bytes 98308
  88.1 25.7 %copy-start.11 = (bf16[1,8,64,32]{2,3,1,0:T(8,128)(2,1)S(1)}, bf16[1,8,64,32]{2,3,1,0:T(8,128)(2,1)}, u32[]{:S(2)}) copy-start(bf16[1,8,64,32]{2,3,1,0:T(8,128)(2,1)} %get-tuple-element.42) | copy-start | bytes 98308
  90.3 25.7 %copy-start.3 = (bf16[1,8,64,32]{2,3,1,0:T(8,128)(2,1)S(1)}, bf16[1,8,64,32]{2,3,1,0:T(8,128)(2,1)}, u32[]{:S(2)}) copy-start(bf16[1,8,64,32]{2,3,1,0:T(8,128)(2,1)} %copy-done.2) | copy-start | bytes 98308
  102.4 16.1 %copy-start.9 = (bf16[1,8,64,32]{2,3,1,0:T(8,128)(2,1)S(1)}, bf16[1,8,64,32]{2,3,1,0:T(8,128)(2,1)}, u32[]{:S(2)}) copy-start(bf16[1,8,64,32]{2,3,1,0:T(8,128)(2,1)} %copy-done.8) | copy-start | bytes 98308
  116.0 5.0 %copy-start.1 = (bf16[1,8,64,32]{2,3,1,0:T(8,128)(2,1)S(1)}, bf16[1,8,64,32]{2,3,1,0:T(8,128)(2,1)}, u32[]{:S(2)}) copy-start(bf16[1,8,64,32]{2,3,1,0:T(8,128)(2,1)} %get-tuple-element.60) | copy-start | bytes 98308
  121.0 5.0 %copy-start.5 = (bf16[1,8,64,32]{2,3,1,0:T(8,128)(2,1)S(1)}, bf16[1,8,64,32]{2,3,1,0:T(8,128)(2,1)}, u32[]{:S(2)}) copy-start(bf16[1,8,64,32]{2,3,1,0:T(8,128)(2,1)} %param.3) | copy-start | bytes 98308
  128.6 5.0 %copy-start.7 = (bf16[1,8,64,32]{2,3,1,0:T(8,128)(2,1)S(1)}, bf16[1,8,64,32]{2,3,1,0:T(8,128)(2,1)}, u32[]{:S(2)}) copy-start(bf16[1,8,64,32]{2,3,1,0:T(8,128)(2,1)} %copy-done.6) | copy-start | bytes 98308
  134.4 3.5 %copy-start.17 = (bf16[512,32]{0,1:T(8,128)(2,1)S(1)}, bf16[512,32]{0,1:T(8,128)(2,1)}, u32[]{:S(2)}) copy-start(bf16[512,32]{0,1:T(8,128)(2,1)} %reshape.324) | copy-start | bytes 98308
  136.9 1.2 copy-start.21
  137.8 0.8 copy-start.25
  137.8 196.1 %reduce-scatter.2.cloned.1.call-start = ((), (), s32[]{:S(2)}) async-start(), calls=%async_computation.1 | async-start | bytes 1179648 | tf_op jit(solution)/shard_map/reduce_scatter | solution.py:36
  138.2 0.8 copy-start.16
  138.6 0.8 copy-start.18
  138.9 0.8 copy-start.19
  139.3 0.8 copy-start.20
  139.7 0.8 copy-start.22
  140.1 0.8 copy-start.23
  140.4 0.8 copy-start.26
  140.9 0.8 copy-start.29
  141.2 0.8 copy-start.15
  141.6 0.8 copy-start.24
  142.0 0.8 copy-start.27
  142.4 0.8 copy-start.28
  142.7 0.8 copy-start.30
  143.2 0.8 copy-start.32
  143.5 0.8 copy-start.33
  143.9 0.8 copy-start.34
  144.3 0.8 copy-start.35
  145.0 0.8 copy-start.31
  145.8 0.8 copy-start.10
  146.8 8.3 %collective-permute-start.7 = (bf16[3,1,64,256]{3,2,1,0:T(8,128)(2,1)S(1)}, bf16[3,1,64,256]{3,2,1,0:T(8,128)(2,1)S(1)}, u32[]{:S(2)}, u32[]{:S(2)}) collective-permute-start(bf16[3,1,64,256]{3,2,1,0:T(8,128)(2,1)S(1)} %get-tuple-element.40), channel_id=1, source_target_pairs={{1,0},{2,1},{3,2},{4,3},{5,4},{6,5},{7,6},{9,8},{10,9},{11,10},{12... | collective-permute-start | bytes 294920 | tf_op jit(solution)/shard_map/ppermute | solution.py:16
  148.7 6.4 %collective-permute-start.6 = (bf16[3,1,64,256]{3,2,1,0:T(8,128)(2,1)S(1)}, bf16[3,1,64,256]{3,2,1,0:T(8,128)(2,1)S(1)}, u32[]{:S(2)}, u32[]{:S(2)}) collective-permute-start(bf16[3,1,64,256]{3,2,1,0:T(8,128)(2,1)S(1)} %get-tuple-element.39), channel_id=1, source_target_pairs={{0,1},{1,2},{2,3},{3,4},{4,5},{5,6},{6,7},{8,9},{9,10},{10,11},{11... | collective-permute-start | bytes 294920 | tf_op jit(solution)/shard_map/ppermute | solution.py:15
Sparse Core Ops, SparseCore 0:
  137.9 193.7 all-reduce.3
Sparse Core Ops, SparseCore 1:
  155.2 32.7 reduce-scatter.1
where the time goes:
time: 345 us; the launch traced here: 343 us
  waiting for transfers between devices  171 us (50%)
  local copies, waits for them, and re-layouts  60 us (17%)
  matrix products  34.2 us (10%)
  starting transfers between devices  29 us (8%)
  blocking collectives  26.2 us (8%)
  between operations  16.2 us (5%)
  other arithmetic  6.23 us (2%)
    psum x1, waiting for transfers between devices, body(): summed = lax.psum(local_kernel, ('sx', 'sy'))  169 us
    reshape x27, local copies, waits for them, and re-layouts, body(): padded[a:a + size_x, b:b + size_y, e:e + size_z].reshape(cells, own_in)  29.3 us
    all_gather x1, blocking collectives, body(): grad_full = lax.all_gather(grad_out, 'chan', axis=3, tiled=True)  26.2 us
    dot_general x27, matrix products, body(): lax.dot_general(in_window, flat_grad, (((0,), (0,)), ((), ())), preferred...  22.6 us
    slice x25, local copies, waits for them, and re-layouts, body(): padded[a:a + size_x, b:b + size_y, e:e + size_z].reshape(cells, own_in)  21 us
    ppermute x4, starting transfers between devices, padded_2(): before = lax.ppermute(last, axis, up)  17.6 us
    ppermute x4, starting transfers between devices, padded_2(): after = lax.ppermute(leading, axis, down)  11.4 us
    unnamed x81, local copies, waits for them, and re-layouts  6.98 us
  transfers between devices with their start and end apart: 10, of which 2 were waited for; matrix products, arithmetic and copies ran while one was open for 28% of the time, Pallas kernels for 0%

commit v1 on v0

--- a/solution.py
+++ b/solution.py
@@ -58,7 +58,7 @@
         )
     grad_input = back.reshape(size_x, size_y, size_z, own_in).astype(jnp.bfloat16)
     local_kernel = jnp.stack(kernel_terms)
-    summed = lax.psum(local_kernel, ("sx", "sy"))
+    summed = lax.psum(lax.psum(local_kernel, "sy"), "sx")
     all_cells = cells * lax.axis_size("sx") * lax.axis_size("sy")
     grad_kernel = summed / jnp.float32(math.sqrt(all_cells))
     return (out, grad_input, grad_kernel)

time: 345 us -> 299 us (0.87)
  the two profiles are of different devices: /device:TPU:25 before, /device:TPU:8 now
where the time goes in v1:
time: 299 us; the launch traced here: 297 us
  waiting for transfers between devices  131 us (44%)
  local copies, waits for them, and re-layouts  58.5 us (20%)
  matrix products  34.2 us (11%)
  blocking collectives  29.5 us (10%)
  starting transfers between devices  21.4 us (7%)
  between operations  16.2 us (5%)
  other arithmetic  6.23 us (2%)
    psum x2, waiting for transfers between devices, body(): summed = lax.psum(lax.psum(local_kernel, 'sy'), 'sx')  128 us
    all_gather x1, blocking collectives, body(): grad_full = lax.all_gather(grad_out, 'chan', axis=3, tiled=True)  29.5 us
    reshape x27, local copies, waits for them, and re-layouts, body(): padded[a:a + size_x, b:b + size_y, e:e + size_z].reshape(cells, own_in)  28.7 us
    dot_general x27, matrix products, body(): lax.dot_general(in_window, flat_grad, (((0,), (0,)), ((), ())), preferred...  22.6 us
    slice x25, local copies, waits for them, and re-layouts, body(): padded[a:a + size_x, b:b + size_y, e:e + size_z].reshape(cells, own_in)  20.1 us
    ppermute x4, starting transfers between devices, padded_2(): after = lax.ppermute(leading, axis, down)  10.9 us
    ppermute x4, starting transfers between devices, padded_2(): before = lax.ppermute(last, axis, up)  10.2 us
    unnamed x81, local copies, waits for them, and re-layouts  6.88 us
  transfers between devices with their start and end apart: 11, of which 4 were waited for; matrix products, arithmetic and copies ran while one was open for 31% of the time, Pallas kernels for 0%

profile of v1, /device:TPU:8, one launch (start us, length us, event | category | flops | bytes accessed | tf_op | source)
XLA Modules:
  0.0 296.7 jit_solution(2149509360669573494)
XLA Ops:
  8.1 1.7 collective-permute-start
  9.8 1.3 collective-permute-start.1
  12.9 1.6 collective-permute-done.1
  14.5 6.0 %collective-permute-start.3 = (bf16[3,1,64,32]{2,3,1,0:T(8,128)(2,1)S(1)}, bf16[3,1,64,32]{2,3,1,0:T(8,128)(2,1)S(1)}, u32[]{:S(2)}, u32[]{:S(2)}) collective-permute-start(bf16[3,1,64,32]{2,3,1,0:T(8,128)(2,1)S(1)} %get-tuple-element.69), channel_id=1, source_target_pairs={{1,0},{2,1},{3,2},{4,3},{5,4},{6,5},{7,6},{9,8},{10,9},{11,10},{12... | collective-permute-start | bytes 36872 | tf_op jit(solution)/shard_map/ppermute | solution.py:16
  20.5 1.9 collective-permute-start.2
  22.4 29.5 %all_gather.3 = bf16[1,8,64,256]{2,1,0,3:T(8,128)(2,1)S(1)} all-gather(bf16[1,8,64,32]{2,1,0,3:T(8,128)(2,1)S(1)} %copy.98), channel_id=1, replica_groups=mesh['chan'=8,'sx'=8,'sy'=8] {'chan'}, dimensions={3}, use_global_device_ids=true | all-gather | bytes 294912 | tf_op jit(solution)/shard_map/all_gather | solution.py:39
  52.3 1.3 collective-permute-start.5
  53.6 3.0 %collective-permute-start.4 = (bf16[1,8,64,256]{3,2,1,0:T(8,128)(2,1)S(1)}, bf16[1,8,64,256]{3,2,1,0:T(8,128)(2,1)S(1)}, u32[]{:S(2)}, u32[]{:S(2)}) collective-permute-start(bf16[1,8,64,256]{3,2,1,0:T(8,128)(2,1)S(1)} %copy.99), channel_id=1, source_target_pairs={{0,8},{8,16},{16,24},{24,32},{32,40},{40,48},{48,56},{1,9},{9,17},... | collective-permute-start | bytes 786440 | tf_op jit(solution)/shard_map/ppermute | solution.py:15
  59.7 1.1 fusion.241
  62.9 1.4 pad_maximum_fusion.13
  65.7 1.5 copy.72
  67.2 1.6 reshape.325
  68.8 1.5 copy.73
  70.3 1.6 reshape.326
  71.8 1.5 copy.76
  73.3 1.6 reshape.329
  74.8 1.5 copy.77
  76.3 1.6 reshape.330
  77.9 1.5 copy.78
  79.4 1.6 reshape.331
  81.6 1.6 reshape.332
  83.8 1.6 reshape.333
  86.0 1.6 reshape.334
  87.6 1.5 copy.82
  89.1 1.6 reshape.335
  90.6 1.5 copy.84
  92.1 1.6 reshape.337
  94.3 1.6 reshape.338
  96.7 1.5 copy.87
  98.2 1.6 reshape.340
  99.7 1.5 copy.88
  101.2 1.6 reshape.341
  103.4 1.6 reshape.342
  105.0 1.5 copy.90
  106.5 1.6 reshape.343
  108.7 1.6 reshape.344
  111.1 0.9 fusion.35
  113.6 0.9 fusion.32
  118.6 0.9 fusion.26
  141.2 2.3 collective-permute-start.7
  143.5 3.5 %collective-permute-start.6 = (bf16[3,1,64,256]{3,2,1,0:T(8,128)(2,1)S(1)}, bf16[3,1,64,256]{3,2,1,0:T(8,128)(2,1)S(1)}, u32[]{:S(2)}, u32[]{:S(2)}) collective-permute-start(bf16[3,1,64,256]{3,2,1,0:T(8,128)(2,1)S(1)} %get-tuple-element.39), channel_id=1, source_target_pairs={{0,1},{1,2},{2,3},{3,4},{4,5},{5,6},{6,7},{8,9},{9,10},{10,11},{11... | collective-permute-start | bytes 294920 | tf_op jit(solution)/shard_map/ppermute | solution.py:15
  147.3 1.3 copy.97
  148.9 1.2 collective-permute-done.6
  150.7 0.9 fusion.240
  156.5 56.5 %all-reduce.5.cloned.1.call-done = f32[27,32,256]{2,1,0:T(8,128)} async-done(((f32[27,32,256]{2,1,0:T(8,128)}), f32[27,32,256]{2,1,0:T(8,128)}) %all-reduce.5.cloned.1.call-update) | async-done | bytes 884752 | tf_op jit(solution)/shard_map/psum | solution.py:61
  214.2 1.5 convert_element_type.21
  215.7 71.4 %all-reduce.7.cloned.1.call-done = f32[27,32,256]{2,1,0:T(8,128)} async-done(((f32[27,32,256]{2,1,0:T(8,128)}), f32[27,32,256]{2,1,0:T(8,128)}) %all-reduce.7.cloned.1.call-update) | async-done | bytes 884752 | tf_op jit(solution)/shard_map/psum | solution.py:61
  287.1 2.2 broadcast_multiply_fusion
  (208 shorter events, 48.2 us)
Async XLA Ops:
  8.0 48.6 %copy-start.4 = (bf16[1,8,64,32]{2,3,1,0:T(8,128)(2,1)S(1)}, bf16[1,8,64,32]{2,3,1,0:T(8,128)(2,1)}, u32[]{:S(2)}) copy-start(bf16[1,8,64,32]{2,3,1,0:T(8,128)(2,1)} %param.3) | copy-start | bytes 98308
  8.0 205.0 %all-reduce.5.cloned.1.call-start = ((), (), s32[]{:S(2)}) async-start(), calls=%async_computation.2 | async-start | bytes 1769472 | tf_op jit(solution)/shard_map/psum | solution.py:61
  8.1 3.9 %collective-permute-start = (bf16[1,8,64,32]{2,3,1,0:T(8,128)(2,1)}, bf16[1,8,64,32]{2,3,1,0:T(8,128)(2,1)S(1)}, u32[]{:S(2)}, u32[]{:S(2)}) collective-permute-start(bf16[1,8,64,32]{2,3,1,0:T(8,128)(2,1)} %param.3), channel_id=1, source_target_pairs={{0,8},{8,16},{16,24},{24,32},{32,40},{40,48},{48,56},{1,9},{9,17},... | collective-permute-start | bytes 98312 | tf_op jit(solution)/shard_map/ppermute | solution.py:15
  9.8 4.6 %collective-permute-start.1 = (bf16[1,8,64,32]{2,3,1,0:T(8,128)(2,1)}, bf16[1,8,64,32]{2,3,1,0:T(8,128)(2,1)S(1)}, u32[]{:S(2)}, u32[]{:S(2)}) collective-permute-start(bf16[1,8,64,32]{2,3,1,0:T(8,128)(2,1)} %param.3), channel_id=1, source_target_pairs={{8,0},{16,8},{24,16},{32,24},{40,32},{48,40},{56,48},{9,1},{17,9},... | collective-permute-start | bytes 98312 | tf_op jit(solution)/shard_map/ppermute | solution.py:16
  12.0 45.5 %copy-start.8 = (bf16[1,8,64,32]{2,3,1,0:T(8,128)(2,1)}, bf16[1,8,64,32]{2,3,1,0:T(8,128)(2,1)S(1)}, u32[]{:S(2)}) copy-start(bf16[1,8,64,32]{2,3,1,0:T(8,128)(2,1)S(1)} %collective-permute-done) | copy-start | bytes 98308
  14.4 43.9 %copy-start.6 = (bf16[1,8,64,32]{2,3,1,0:T(8,128)(2,1)}, bf16[1,8,64,32]{2,3,1,0:T(8,128)(2,1)S(1)}, u32[]{:S(2)}) copy-start(bf16[1,8,64,32]{2,3,1,0:T(8,128)(2,1)S(1)} %collective-permute-done.1) | copy-start | bytes 98308
  14.5 43.9 %collective-permute-start.3 = (bf16[3,1,64,32]{2,3,1,0:T(8,128)(2,1)S(1)}, bf16[3,1,64,32]{2,3,1,0:T(8,128)(2,1)S(1)}, u32[]{:S(2)}, u32[]{:S(2)}) collective-permute-start(bf16[3,1,64,32]{2,3,1,0:T(8,128)(2,1)S(1)} %get-tuple-element.69), channel_id=1, source_target_pairs={{1,0},{2,1},{3,2},{4,3},{5,4},{6,5},{7,6},{9,8},{10,9},{11,10},{12... | collective-permute-start | bytes 36872 | tf_op jit(solution)/shard_map/ppermute | solution.py:16
  20.5 37.9 %collective-permute-start.2 = (bf16[3,1,64,32]{2,3,1,0:T(8,128)(2,1)S(1)}, bf16[3,1,64,32]{2,3,1,0:T(8,128)(2,1)S(1)}, u32[]{:S(2)}, u32[]{:S(2)}) collective-permute-start(bf16[3,1,64,32]{2,3,1,0:T(8,128)(2,1)S(1)} %get-tuple-element.68), channel_id=1, source_target_pairs={{0,1},{1,2},{2,3},{3,4},{4,5},{5,6},{6,7},{8,9},{9,10},{10,11},{11... | collective-permute-start | bytes 36872 | tf_op jit(solution)/shard_map/ppermute | solution.py:15
  52.3 88.8 %collective-permute-start.5 = (bf16[1,8,64,256]{3,2,1,0:T(8,128)(2,1)S(1)}, bf16[1,8,64,256]{3,2,1,0:T(8,128)(2,1)S(1)}, u32[]{:S(2)}, u32[]{:S(2)}) collective-permute-start(bf16[1,8,64,256]{3,2,1,0:T(8,128)(2,1)S(1)} %copy.99), channel_id=1, source_target_pairs={{8,0},{16,8},{24,16},{32,24},{40,32},{48,40},{56,48},{9,1},{17,9},... | collective-permute-start | bytes 786440 | tf_op jit(solution)/shard_map/ppermute | solution.py:16
  53.6 87.5 %collective-permute-start.4 = (bf16[1,8,64,256]{3,2,1,0:T(8,128)(2,1)S(1)}, bf16[1,8,64,256]{3,2,1,0:T(8,128)(2,1)S(1)}, u32[]{:S(2)}, u32[]{:S(2)}) collective-permute-start(bf16[1,8,64,256]{3,2,1,0:T(8,128)(2,1)S(1)} %copy.99), channel_id=1, source_target_pairs={{0,8},{8,16},{16,24},{24,32},{32,40},{40,48},{48,56},{1,9},{9,17},... | collective-permute-start | bytes 786440 | tf_op jit(solution)/shard_map/ppermute | solution.py:15
  58.3 0.6 copy-start.36
  59.7 2.3 copy-start
  64.3 0.6 copy-start.2
  64.3 16.6 %copy-start.15 = (bf16[1,8,64,32]{2,3,1,0:T(8,128)(2,1)S(1)}, bf16[1,8,64,32]{2,3,1,0:T(8,128)(2,1)}, u32[]{:S(2)}) copy-start(bf16[1,8,64,32]{2,3,1,0:T(8,128)(2,1)} %get-tuple-element.52) | copy-start | bytes 98308
  64.3 21.0 %copy-start.14 = (bf16[1,8,64,32]{2,3,1,0:T(8,128)(2,1)S(1)}, bf16[1,8,64,32]{2,3,1,0:T(8,128)(2,1)}, u32[]{:S(2)}) copy-start(bf16[1,8,64,32]{2,3,1,0:T(8,128)(2,1)} %get-tuple-element.51) | copy-start | bytes 98308
  67.2 26.5 %copy-start.13 = (bf16[1,8,64,32]{2,3,1,0:T(8,128)(2,1)S(1)}, bf16[1,8,64,32]{2,3,1,0:T(8,128)(2,1)}, u32[]{:S(2)}) copy-start(bf16[1,8,64,32]{2,3,1,0:T(8,128)(2,1)} %get-tuple-element.48) | copy-start | bytes 98308
  83.8 24.3 %copy-start.12 = (bf16[1,8,64,32]{2,3,1,0:T(8,128)(2,1)S(1)}, bf16[1,8,64,32]{2,3,1,0:T(8,128)(2,1)}, u32[]{:S(2)}) copy-start(bf16[1,8,64,32]{2,3,1,0:T(8,128)(2,1)} %get-tuple-element.44) | copy-start | bytes 98308
  86.0 24.3 %copy-start.3 = (bf16[1,8,64,32]{2,3,1,0:T(8,128)(2,1)S(1)}, bf16[1,8,64,32]{2,3,1,0:T(8,128)(2,1)}, u32[]{:S(2)}) copy-start(bf16[1,8,64,32]{2,3,1,0:T(8,128)(2,1)} %copy-done.2) | copy-start | bytes 98308
  96.7 16.1 %copy-start.9 = (bf16[1,8,64,32]{2,3,1,0:T(8,128)(2,1)S(1)}, bf16[1,8,64,32]{2,3,1,0:T(8,128)(2,1)}, u32[]{:S(2)}) copy-start(bf16[1,8,64,32]{2,3,1,0:T(8,128)(2,1)} %copy-done.8) | copy-start | bytes 98308
  108.7 6.6 %copy-start.1 = (bf16[1,8,64,32]{2,3,1,0:T(8,128)(2,1)S(1)}, bf16[1,8,64,32]{2,3,1,0:T(8,128)(2,1)}, u32[]{:S(2)}) copy-start(bf16[1,8,64,32]{2,3,1,0:T(8,128)(2,1)} %get-tuple-element.60) | copy-start | bytes 98308
  115.3 5.0 %copy-start.5 = (bf16[1,8,64,32]{2,3,1,0:T(8,128)(2,1)S(1)}, bf16[1,8,64,32]{2,3,1,0:T(8,128)(2,1)}, u32[]{:S(2)}) copy-start(bf16[1,8,64,32]{2,3,1,0:T(8,128)(2,1)} %param.3) | copy-start | bytes 98308
  122.8 5.0 %copy-start.7 = (bf16[1,8,64,32]{2,3,1,0:T(8,128)(2,1)S(1)}, bf16[1,8,64,32]{2,3,1,0:T(8,128)(2,1)}, u32[]{:S(2)}) copy-start(bf16[1,8,64,32]{2,3,1,0:T(8,128)(2,1)} %copy-done.6) | copy-start | bytes 98308
  128.7 3.5 %copy-start.18 = (bf16[512,32]{0,1:T(8,128)(2,1)S(1)}, bf16[512,32]{0,1:T(8,128)(2,1)}, u32[]{:S(2)}) copy-start(bf16[512,32]{0,1:T(8,128)(2,1)} %reshape.324) | copy-start | bytes 98308
  131.2 1.2 copy-start.22
  132.1 0.8 copy-start.26
  132.1 82.1 %reduce-scatter.2.cloned.1.call-start = ((), (), s32[]{:S(2)}) async-start(), calls=%async_computation.1 | async-start | bytes 1179648 | tf_op jit(solution)/shard_map/reduce_scatter | solution.py:36
  132.4 0.8 copy-start.17
  132.9 0.8 copy-start.19
  133.2 0.8 copy-start.20
  133.6 0.8 copy-start.21
  134.0 0.8 copy-start.23
  134.4 0.8 copy-start.24
  134.7 0.8 copy-start.27
  135.1 0.8 copy-start.30
  135.5 0.8 copy-start.16
  135.9 0.8 copy-start.25
  136.2 0.8 copy-start.28
  136.7 0.8 copy-start.29
  137.0 0.8 copy-start.31
  137.4 0.8 copy-start.32
  137.8 0.8 copy-start.33
  138.2 0.8 copy-start.34
  138.5 0.8 copy-start.35
  139.3 0.8 copy-start.11
  139.8 0.9 copy-start.10
  141.2 7.7 %collective-permute-start.7 = (bf16[3,1,64,256]{3,2,1,0:T(8,128)(2,1)S(1)}, bf16[3,1,64,256]{3,2,1,0:T(8,128)(2,1)S(1)}, u32[]{:S(2)}, u32[]{:S(2)}) collective-permute-start(bf16[3,1,64,256]{3,2,1,0:T(8,128)(2,1)S(1)} %get-tuple-element.40), channel_id=1, source_target_pairs={{1,0},{2,1},{3,2},{4,3},{5,4},{6,5},{7,6},{9,8},{10,9},{11,10},{12... | collective-permute-start | bytes 294920 | tf_op jit(solution)/shard_map/ppermute | solution.py:16
  143.5 6.5 %collective-permute-start.6 = (bf16[3,1,64,256]{3,2,1,0:T(8,128)(2,1)S(1)}, bf16[3,1,64,256]{3,2,1,0:T(8,128)(2,1)S(1)}, u32[]{:S(2)}, u32[]{:S(2)}) collective-permute-start(bf16[3,1,64,256]{3,2,1,0:T(8,128)(2,1)S(1)} %get-tuple-element.39), channel_id=1, source_target_pairs={{0,1},{1,2},{2,3},{3,4},{4,5},{5,6},{6,7},{8,9},{9,10},{10,11},{11... | collective-permute-start | bytes 294920 | tf_op jit(solution)/shard_map/ppermute | solution.py:15
  148.6 138.5 %all-reduce.7.cloned.1.call-start = ((), (), s32[]{:S(2)}) async-start(), calls=%async_computation.3 | async-start | bytes 1769472 | tf_op jit(solution)/shard_map/psum | solution.py:61
  (1 other events, 0.6 us)
Sparse Core Ops, SparseCore 0:
  132.2 80.7 all-reduce.4
  215.5 71.5 all-reduce.6
Sparse Core Ops, SparseCore 1:
  148.7 42.0 reduce-scatter.1
